TPU v7x, 512 devices: a whole 4x8x8 slice. The times are simulated.
512 devices in a mesh: grp: 16 (over z, core), dom: 32 (over x, y).
Axes of the slice: x: 4, y: 8, z: 8, core: 2. Of those that a mesh axis runs over, the one named last changes fastest.
Arguments:
- leaf_load: bfloat16 [32, 16, 1024, 128], P('dom', 'grp'), may hold values from -6 to 6
- leaf_map: bfloat16 [32, 16, 1024, 1024], P('dom', 'grp'), may hold values from -0.1875 to 0.1875
- group_map: bfloat16 [32, 4096, 4096], P('dom', 'grp'), may hold values from -0.09375 to 0.09375
- node_index: int32 [32, 16, 1024], P('dom', 'grp'), may hold values from 0 to 4095, as said below
- west_coupling: float32 [32, 256, 256], P('dom'), may hold values from -1.5 to 1.5
- east_coupling: float32 [32, 256, 256], P('dom'), may hold values from -1.5 to 1.5
Outputs:
- leaf_solution: bfloat16 [32, 16, 1024, 128], P('dom', 'grp')
Inputs may be any that keep to these rules, and one draw needn't show every extreme that they name: `node_index`: each leaf's list names 1024 different interface nodes of its group.
All inputs are finite; a program needn't handle non-finite values.
Results may differ from a plain program's by a relative error of at most 0.015.
Values may be sent and summed in bfloat16 or wider, within the bound.
No kernel may reach another device: no remote copies, remote signals or barrier semaphores. Data moves between devices by JAX's collectives and lax.ppermute only.
A program may use at most 128 MiB of HBM per device.

v0:
```python
import jax
import jax.numpy as jnp
from jax import lax
from jax.sharding import PartitionSpec as P


def carried_in(part, axis, combine, identity, reverse):
    count = lax.axis_size(axis)
    place = lax.axis_index(axis)
    ahead = count - 1 - place if reverse else place
    gathered = jax.tree.map(lambda a: lax.all_gather(a, axis), part)
    state = jax.tree.map(lambda a, e: jnp.zeros_like(a) + jnp.asarray(e, a.dtype), part, identity)

    def one(turn, state):
        source = count - 1 - turn if reverse else turn
        return combine(
            state, jax.tree.map(lambda a: lax.dynamic_index_in_dim(a, source, 0, False), gathered)
        )

    return lax.fori_loop(0, ahead, one, state)


def compose(earlier, follower):
    early_map, early_value = earlier
    late_map, late_value = follower
    joined_map = jnp.dot(
        late_map, early_map, precision=lax.Precision.HIGHEST, preferred_element_type=jnp.float32
    )
    joined_value = (
        jnp.dot(
            late_map,
            early_value,
            precision=lax.Precision.HIGHEST,
            preferred_element_type=jnp.float32,
        )
        + late_value
    )
    return (joined_map, joined_value)


def on_device(leaf_load, leaf_map, group_map, node_index, west_coupling, east_coupling):
    exact_mode = lax.Precision.HIGHEST
    columns = leaf_load.shape[3]
    interface = group_map.shape[2]
    face_nodes = west_coupling.shape[1]
    stride = interface // face_nodes
    local_map = leaf_map[0, 0]
    local_load = leaf_load[0, 0]
    local_index = node_index[0, 0]
    contrib = jnp.dot(local_map, local_load, preferred_element_type=jnp.float32).astype(
        jnp.bfloat16
    )
    scattered = (
        jnp.zeros((interface, columns), jnp.float32)
        .at[local_index]
        .add(contrib.astype(jnp.float32))
    )
    summed_loads = lax.psum(scattered.astype(jnp.bfloat16), "grp")
    rows_map = group_map[0]
    row_count = rows_map.shape[0]
    blocks = row_count // stride
    initial_rows = jnp.dot(rows_map, summed_loads, preferred_element_type=jnp.float32)
    block_view = rows_map.reshape(blocks, stride, face_nodes, stride)
    column_view = rows_map.reshape(row_count, face_nodes, stride)
    west_columns = column_view[:, :, 0].astype(jnp.float32)
    east_columns = column_view[:, :, 1].astype(jnp.float32)
    east_west = block_view[:, 1, :, 0].astype(jnp.float32)
    west_east = block_view[:, 0, :, 1].astype(jnp.float32)
    identity_map = jnp.eye(face_nodes, dtype=jnp.float32)
    zero_values = jnp.zeros((face_nodes, columns), jnp.float32)
    forward_maps = jnp.dot(east_west, west_coupling[0], precision=exact_mode)
    east_values = initial_rows.reshape(blocks, stride, columns)[:, 1]
    face_maps, face_values = (
        lax.all_gather(forward_maps, "grp", axis=0, tiled=True),
        lax.all_gather(east_values, "grp", axis=0, tiled=True),
    )
    _, incoming = carried_in(
        (face_maps, face_values), "dom", compose, (identity_map, zero_values), False
    )
    swept_rows = initial_rows + jnp.dot(
        west_columns,
        jnp.dot(west_coupling[0], incoming, precision=exact_mode),
        precision=exact_mode,
    )
    backward_maps = jnp.dot(west_east, east_coupling[0], precision=exact_mode)
    west_values = swept_rows.reshape(blocks, stride, columns)[:, 0]
    back_maps, back_values = (
        lax.all_gather(backward_maps, "grp", axis=0, tiled=True),
        lax.all_gather(west_values, "grp", axis=0, tiled=True),
    )
    _, outgoing = carried_in(
        (back_maps, back_values), "dom", compose, (identity_map, zero_values), True
    )
    final_rows = swept_rows + jnp.dot(
        east_columns,
        jnp.dot(east_coupling[0], outgoing, precision=exact_mode),
        precision=exact_mode,
    )
    gathered = lax.all_gather(final_rows.astype(jnp.bfloat16), "grp", axis=0, tiled=True)
    picked = gathered[local_index]
    result = lax.dot_general(
        local_map, picked, (((0,), (0,)), ((), ())), preferred_element_type=jnp.float32
    )
    result = result + local_load.astype(jnp.float32)
    return result.astype(jnp.bfloat16)[None, None]


def solution(mesh):
    return jax.shard_map(
        on_device,
        mesh=mesh,
        in_specs=(
            P("dom", "grp", None, None),
            P("dom", "grp", None, None),
            P("dom", "grp", None),
            P("dom", "grp", None),
            P("dom", None, None),
            P("dom", None, None),
        ),
        out_specs=P("dom", "grp", None, None),
        check_vma=False,
    )
```

profile of v0, /device:TPU:1, one launch (start us, length us, event | category | flops | bytes accessed | tf_op | source)
XLA Modules:
  0.0 639.1 jit_solution(5721224680582235260)
XLA Ops:
  6.5 0.8 compare_select_fusion
  7.4 0.8 copy-done
  8.1 1.6 fusion.21
  9.8 7.4 %scatter_custom_fusion = f32[4096,128]{1,0:T(8,128)} fusion(s32[1024]{0:T(1024)S(1)} %bitcast.114, f32[1024,128]{1,0:T(8,128)S(1)} %fusion.21, f32[]{:T(128)} %constant.56.clone.1), kind=kCustom, calls=%fused_computation.30 | custom fusion | flops 131072 | bytes 2097156 | tf_op jit(solution)/shard_map/scatter-add | solution.py:56
  17.2 2.7 convert_element_type.25
  20.0 123.9 %all-reduce.2.cloned.1.call-done = bf16[4096,128]{1,0:T(8,128)(2,1)} async-done(((bf16[4096,128]{1,0:T(8,128)(2,1)}), bf16[4096,128]{1,0:T(8,128)(2,1)}) %all-reduce.2.cloned.1.call-update) | async-done | bytes 1048592 | tf_op jit(solution)/shard_map/psum | solution.py:58
  143.9 2.7 fusion.30
  146.8 16.8 %all-gather.1 = f32[256,1,128]{2,1,0:T(1,128)} all-gather(f32[16,1,128]{2,1,0:T(1,128)S(1)} %slice.27), channel_id=3, replica_groups=mesh['grp'=16,'dom'=32] {'grp'}, dimensions={0}, use_global_device_ids=true | all-gather | bytes 139264 | tf_op jit(solution)/shard_map/all_gather | solution.py:75
  163.6 16.8 %reshape_squeeze.6 = bf16[16,16,256,16]{3,2,1,0:T(8,128)(2,1)} reshape(bf16[1,256,4096]{2,1,0:T(8,128)(2,1)} %param.12) | data formatting | bytes 4194304 | tf_op jit(solution)/shard_map/reshape;squeeze | solution.py:63
  180.4 2.6 slice_reduce_fusion
  183.0 0.2 fusion.45
  183.2 18.9 %all_gather.39 = f32[256,256]{1,0:T(8,128)} all-gather(f32[16,256]{1,0:T(8,128)S(1)} %fusion.45), channel_id=1, replica_groups=mesh['grp'=16,'dom'=32] {'grp'}, dimensions={0}, use_global_device_ids=true | all-gather | bytes 278528 | tf_op jit(solution)/shard_map/all_gather | solution.py:74
  202.2 0.2 fusion.41
  202.4 16.7 %all_gather.45 = f32[256,256]{1,0:T(8,128)} all-gather(f32[16,256]{1,0:T(8,128)S(1)} %fusion.41), channel_id=1, replica_groups=mesh['grp'=16,'dom'=32] {'grp'}, dimensions={0}, use_global_device_ids=true | all-gather | bytes 278528 | tf_op jit(solution)/shard_map/all_gather | solution.py:88
  219.2 4.1 copy.22
  223.3 2.0 fusion.49
  225.5 21.1 %all-gather.16.cloned.1.call-done = f32[8192,1,128]{2,1,0:T(1,128)} async-done(((f32[256,1,128]{2,1,0:T(1,128)}), f32[8192,1,128]{2,1,0:T(1,128)}) %all-gather.16.cloned.1.call-update) | async-done | bytes 4194320 | tf_op jit(solution)/shard_map/all_gather | solution.py:11
  246.6 106.2 %all-gather.14.cloned.1.call-done = f32[8192,256]{1,0:T(8,128)} async-done(((f32[256,256]{1,0:T(8,128)}), f32[8192,256]{1,0:T(8,128)}) %all-gather.14.cloned.1.call-update) | async-done | bytes 8388624 | tf_op jit(solution)/shard_map/all_gather | solution.py:11
  352.8 0.4 fusion.43
  353.2 0.3 fusion.33
  353.6 21.1 %all-gather.4 = f32[256,1,128]{2,1,0:T(1,128)} all-gather(f32[16,1,128]{2,1,0:T(1,128)S(1)} %slice.30), channel_id=6, replica_groups=mesh['grp'=16,'dom'=32] {'grp'}, dimensions={0}, use_global_device_ids=true | all-gather | bytes 139264 | tf_op jit(solution)/shard_map/all_gather | solution.py:89
  374.7 0.1 copy.25
  374.9 81.4 %all-gather.18.cloned.1.call-done = f32[8192,256]{1,0:T(8,128)} async-done(((f32[256,256]{1,0:T(8,128)}), f32[8192,256]{1,0:T(8,128)}) %all-gather.18.cloned.1.call-update) | async-done | bytes 8388624 | tf_op jit(solution)/shard_map/all_gather | solution.py:11
  456.3 84.8 %all-gather.20.cloned.1.call-done = f32[8192,1,128]{2,1,0:T(1,128)} async-done(((f32[256,1,128]{2,1,0:T(1,128)}), f32[8192,1,128]{2,1,0:T(1,128)}) %all-gather.20.cloned.1.call-update) | async-done | bytes 4194320 | tf_op jit(solution)/shard_map/all_gather | solution.py:11
  541.1 43.8 %while.27 = (s32[]{:T(128)}, f32[256,128]{1,0:T(8,128)S(1)}, s32[]{:T(128)}, f32[32,256,256]{2,1,0:T(8,128)}, f32[32,256,128]{2,1,0:T(8,128)}, /*index=5*/s32[]{:T(128)}, s32[]{:T(128)}, s32[]{:T(128)}, s32[]{:T(128)}) while((s32[]{:T(128)}, f32[256,128]{1,0:T(8,128)S(1)}, s32[]{:T(128)}, f32[32,256,256]{2,1,0:T(8,128)}, ...), condition=%wide.region_5.6_spmd, body=%wide.region_4.5_spmd.sunk | while | flops 100696072 | bytes 918675 | solution.py:20
  541.1 1.4 convolution_add_fusion.5
  542.6 1.4 convolution_add_fusion.5
  544.0 1.4 convolution_add_fusion.5
  545.4 1.4 convolution_add_fusion.5
  546.8 1.4 convolution_add_fusion.5
  548.2 1.4 convolution_add_fusion.5
  549.6 1.4 convolution_add_fusion.5
  551.1 1.4 convolution_add_fusion.5
  552.5 1.4 convolution_add_fusion.5
  553.9 1.4 convolution_add_fusion.5
  555.3 1.4 convolution_add_fusion.5
  556.7 1.4 convolution_add_fusion.5
  558.1 1.4 convolution_add_fusion.5
  559.5 1.4 convolution_add_fusion.5
  560.9 1.4 convolution_add_fusion.5
  562.3 1.4 convolution_add_fusion.5
  563.8 1.4 convolution_add_fusion.5
  565.2 1.4 convolution_add_fusion.5
  566.6 1.4 convolution_add_fusion.5
  568.0 1.4 convolution_add_fusion.5
  569.4 1.4 convolution_add_fusion.5
  570.8 1.4 convolution_add_fusion.5
  572.2 1.4 convolution_add_fusion.5
  573.6 1.4 convolution_add_fusion.5
  575.1 1.4 convolution_add_fusion.5
  576.5 1.4 convolution_add_fusion.5
  577.9 1.4 convolution_add_fusion.5
  579.3 1.4 convolution_add_fusion.5
  580.7 1.4 convolution_add_fusion.5
  582.1 1.4 convolution_add_fusion.5
  583.5 1.4 convolution_add_fusion.5
  584.9 0.4 fusion.39
  585.3 0.9 fusion.35
  586.3 0.9 copy.20
  587.1 38.1 %all-gather.12.cloned.1.call-done = bf16[4096,128]{0,1:T(8,128)(2,1)} async-done(((bf16[256,128]{0,1:T(8,128)(2,1)}), bf16[4096,128]{0,1:T(8,128)(2,1)}) %all-gather.12.cloned.1.call-update) | async-done | bytes 1048592 | tf_op jit(solution)/shard_map/all_gather | solution.py:99
  625.2 1.6 copy.26
  626.8 3.2 gather_fusion
  630.0 1.4 fusion.27
  631.5 0.8 copy.27
  (59 shorter events, 1.0 us)
Async XLA Ops:
  6.5 1.6 copy-start
  6.5 137.4 %all-reduce.2.cloned.1.call-start = ((), (), s32[]{:S(2)}) async-start(), calls=%async_computation | async-start | bytes 2097152 | tf_op jit(solution)/shard_map/psum | solution.py:58
  19.9 226.7 %all-gather.16.cloned.1.call-start = ((), (), s32[]{:S(2)}) async-start(), calls=%async_computation.3 | async-start | bytes 4325376 | tf_op jit(solution)/shard_map/all_gather | solution.py:11
  163.5 189.2 %all-gather.14.cloned.1.call-start = ((), (), s32[]{:S(2)}) async-start(), calls=%async_computation.2 | async-start | bytes 8650752 | tf_op jit(solution)/shard_map/all_gather | solution.py:11
  180.4 2.6 copy-start.1
  180.4 21.8 %copy-start.2 = (f32[1,256,256]{2,1,0:T(8,128)S(1)}, f32[1,256,256]{2,1,0:T(8,128)}, u32[]{:S(2)}) copy-start(f32[1,256,256]{2,1,0:T(8,128)} %param.15) | copy-start | bytes 786436
  202.1 254.1 %all-gather.18.cloned.1.call-start = ((), (), s32[]{:S(2)}) async-start(), calls=%async_computation.4 | async-start | bytes 8650752 | tf_op jit(solution)/shard_map/all_gather | solution.py:11
  219.1 321.9 %all-gather.20.cloned.1.call-start = ((), (), s32[]{:S(2)}) async-start(), calls=%async_computation.5 | async-start | bytes 4325376 | tf_op jit(solution)/shard_map/all_gather | solution.py:11
  374.7 250.5 %all-gather.12.cloned.1.call-start = ((), (), s32[]{:S(2)}) async-start(), calls=%async_computation.1 | async-start | bytes 1114112 | tf_op jit(solution)/shard_map/all_gather | solution.py:99
  541.1 45.2 %copy-start.3 = (bf16[1,1,1024,128]{3,2,1,0:T(8,128)(2,1)S(1)}, bf16[1,1,1024,128]{3,2,1,0:T(8,128)(2,1)}, u32[]{:S(2)}) copy-start(bf16[1,1,1024,128]{3,2,1,0:T(8,128)(2,1)} %param.10) | copy-start | bytes 786436
Sparse Core Ops, SparseCore 0:
  20.0 123.8 all-reduce.1
  163.7 82.8 all-gather.15
  249.8 102.9 all-gather.13
  355.8 100.4 all-gather.17
  459.3 81.7 all-gather.19
  586.4 38.7 all-gather.11
where the time goes:
time: 641 us; the launch traced here: 639 us
  waiting for transfers between devices  456 us (71%)
  blocking collectives  73.4 us (11%)
  matrix products  50.6 us (8%)
  local copies, waits for them, and re-layouts  33.6 us (5%)
  between operations  13.6 us (2%)
  other arithmetic  10.9 us (2%)
    all_gather x4, waiting for transfers between devices, carried_in(): gathered = jax.tree.map(lambda a: lax.all_gather(a, axis), part)  293 us
    psum x1, waiting for transfers between devices, on_device(): summed_loads = lax.psum(scattered.astype(jnp.bfloat16), 'grp')  124 us
    dot_general x31, matrix products, compose(): jnp.dot(late_map, early_value, precision=lax.Precision.HIGHEST, preferred...  42.3 us
    all_gather x1, waiting for transfers between devices, on_device(): lax.all_gather(final_rows.astype(jnp.bfloat16), 'grp', axis=0, tiled=True)  38.1 us
    all_gather x1, blocking collectives, on_device(): lax.all_gather(west_values, 'grp', axis=0, tiled=True)  21.1 us
    all_gather x1, blocking collectives, on_device(): lax.all_gather(forward_maps, 'grp', axis=0, tiled=True)  18.9 us
    another operation x1, local copies, waits for them, and re-layouts, on_device(): block_view = rows_map.reshape(blocks, stride, face_nodes, stride)  16.8 us
    all_gather x1, blocking collectives, on_device(): lax.all_gather(east_values, 'grp', axis=0, tiled=True)  16.8 us
  transfers between devices with their start and end apart: 6, of which 6 were waited for; matrix products, arithmetic and copies ran while one was open for 4% of the time, Pallas kernels for 0%

commit v1 on v0

--- a/solution.py
+++ b/solution.py
@@ -55,7 +55,9 @@
         .at[local_index]
         .add(contrib.astype(jnp.float32))
     )
-    summed_loads = lax.psum(scattered.astype(jnp.bfloat16), "grp")
+    own = scattered.astype(jnp.bfloat16)
+    parts = lax.all_gather(own, "grp", axis=0, tiled=False)
+    summed_loads = parts.sum(axis=0)
     rows_map = group_map[0]
     row_count = rows_map.shape[0]
     blocks = row_count // stride

time: 641 us -> 604 us (0.942)
  waiting for transfers between devices: 456 us -> 397 us
  blocking collectives: 73.4 us -> 86.5 us
  other arithmetic: 10.9 us -> 19.9 us
    psum x1 -> x0, waiting for transfers between devices: 124 us -> none  [on_device(): summed_loads = lax.psum(scattered.astype(jnp.bfloat16), 'grp')]
    all_gather x0 -> x1, waiting for transfers between devices: none -> 58 us  [on_device(): parts = lax.all_gather(own, 'grp', axis=0, tiled=False)]
    all_gather x1, blocking collectives: 18.9 us -> 28.5 us  [on_device(): lax.all_gather(forward_maps, 'grp', axis=0, tiled=True)]
    reduce_sum x0 -> x1, other arithmetic: none -> 8.87 us  [on_device(): summed_loads = parts.sum(axis=0)]
    all_gather x4, waiting for transfers between devices: 293 us -> 301 us  [carried_in(): gathered = jax.tree.map(lambda a: lax.all_gather(a, axis), part)]
  transfers between devices with their start and end apart: 6 -> 6, of which waited for: 6 -> 6; matrix products, arithmetic and copies ran while one was open for 4% -> 7% of each run, Pallas kernels for 0% -> 0%
where the time goes in v1:
time: 604 us; the launch traced here: 603 us
  waiting for transfers between devices  397 us (66%)
  blocking collectives  86.5 us (14%)
  matrix products  51.2 us (8%)
  local copies, waits for them, and re-layouts  33.5 us (6%)
  other arithmetic  19.9 us (3%)
  between operations  13.7 us (2%)
    all_gather x4, waiting for transfers between devices, carried_in(): gathered = jax.tree.map(lambda a: lax.all_gather(a, axis), part)  301 us
    all_gather x1, waiting for transfers between devices, on_device(): parts = lax.all_gather(own, 'grp', axis=0, tiled=False)  58 us
    dot_general x31, matrix products, compose(): jnp.dot(late_map, early_value, precision=lax.Precision.HIGHEST, preferred...  42.4 us
    all_gather x1, waiting for transfers between devices, on_device(): lax.all_gather(final_rows.astype(jnp.bfloat16), 'grp', axis=0, tiled=True)  38.1 us
    all_gather x1, blocking collectives, on_device(): lax.all_gather(forward_maps, 'grp', axis=0, tiled=True)  28.5 us
    all_gather x1, blocking collectives, on_device(): lax.all_gather(west_values, 'grp', axis=0, tiled=True)  23.8 us
    all_gather x1, blocking collectives, on_device(): lax.all_gather(east_values, 'grp', axis=0, tiled=True)  17.2 us
    all_gather x1, blocking collectives, on_device(): lax.all_gather(backward_maps, 'grp', axis=0, tiled=True)  17 us
  transfers between devices with their start and end apart: 6, of which 6 were waited for; matrix products, arithmetic and copies ran while one was open for 7% of the time, Pallas kernels for 0%

profile of v1, /device:TPU:1, one launch (start us, length us, event | category | flops | bytes accessed | tf_op | source)
XLA Modules:
  0.0 603.0 jit_solution(3223060665985337164)
XLA Ops:
  6.5 0.8 compare_select_fusion
  7.4 0.8 copy-done
  8.1 1.6 fusion.21
  9.8 7.4 %scatter_custom_fusion = f32[4096,128]{1,0:T(8,128)} fusion(s32[1024]{0:T(1024)S(1)} %bitcast.116, f32[1024,128]{1,0:T(8,128)S(1)} %fusion.21, f32[]{:T(128)} %constant.58.clone.1), kind=kCustom, calls=%fused_computation.30 | custom fusion | flops 131072 | bytes 2097156 | tf_op jit(solution)/shard_map/scatter-add | solution.py:56
  17.2 2.7 convert_element_type.27
  20.0 16.8 %reshape_squeeze.6 = bf16[16,16,256,16]{3,2,1,0:T(8,128)(2,1)} reshape(bf16[1,256,4096]{2,1,0:T(8,128)(2,1)} %param.12) | data formatting | bytes 4194304 | tf_op jit(solution)/shard_map/reshape;squeeze | solution.py:65
  36.8 2.6 slice_reduce_fusion
  39.4 0.2 fusion.45
  39.6 28.5 %all_gather.47 = f32[256,256]{1,0:T(8,128)} all-gather(f32[16,256]{1,0:T(8,128)S(1)} %fusion.45), channel_id=1, replica_groups=mesh['grp'=16,'dom'=32] {'grp'}, dimensions={0}, use_global_device_ids=true | all-gather | bytes 278528 | tf_op jit(solution)/shard_map/all_gather | solution.py:76
  68.1 58.0 %all-gather.16.cloned.1.call-done = bf16[65536,128]{1,0:T(8,128)(2,1)} async-done(((bf16[4096,128]{1,0:T(8,128)(2,1)}), bf16[65536,128]{1,0:T(8,128)(2,1)}) %all-gather.16.cloned.1.call-update) | async-done | bytes 16777232 | tf_op jit(solution)/shard_map/all_gather | solution.py:59
  126.2 8.9 %reduce_sum.12 = bf16[4096,128]{1,0:T(8,128)(2,1)S(1)} reduce(bf16[16,4096,128]{2,1,0:T(8,128)(2,1)} %bitcast.108, bf16[]{:T(256)} %constant.61.clone.1), dimensions={0}, to_apply=%region_1.0 | reduce | flops 7864320 | bytes 17825794 | tf_op jit(solution)/shard_map/reduce_sum | solution.py:60
  135.1 2.4 fusion.30
  137.6 17.2 %all-gather.2 = f32[256,1,128]{2,1,0:T(1,128)} all-gather(f32[16,1,128]{2,1,0:T(1,128)S(1)} %slice.27), channel_id=4, replica_groups=mesh['grp'=16,'dom'=32] {'grp'}, dimensions={0}, use_global_device_ids=true | all-gather | bytes 139264 | tf_op jit(solution)/shard_map/all_gather | solution.py:77
  154.9 1.2 fusion.41
  156.1 17.0 %all_gather.53 = f32[256,256]{1,0:T(8,128)} all-gather(f32[16,256]{1,0:T(8,128)S(1)} %fusion.41), channel_id=1, replica_groups=mesh['grp'=16,'dom'=32] {'grp'}, dimensions={0}, use_global_device_ids=true | all-gather | bytes 278528 | tf_op jit(solution)/shard_map/all_gather | solution.py:90
  173.1 4.1 copy.30
  177.2 2.0 fusion.49
  179.3 49.8 %all-gather.18.cloned.1.call-done = f32[8192,256]{1,0:T(8,128)} async-done(((f32[256,256]{1,0:T(8,128)}), f32[8192,256]{1,0:T(8,128)}) %all-gather.18.cloned.1.call-update) | async-done | bytes 8388624 | tf_op jit(solution)/shard_map/all_gather | solution.py:11
  229.1 84.9 %all-gather.20.cloned.1.call-done = f32[8192,1,128]{2,1,0:T(1,128)} async-done(((f32[256,1,128]{2,1,0:T(1,128)}), f32[8192,1,128]{2,1,0:T(1,128)}) %all-gather.20.cloned.1.call-update) | async-done | bytes 4194320 | tf_op jit(solution)/shard_map/all_gather | solution.py:11
  314.1 0.4 fusion.43
  314.5 0.3 fusion.33
  314.9 23.8 %all-gather.5 = f32[256,1,128]{2,1,0:T(1,128)} all-gather(f32[16,1,128]{2,1,0:T(1,128)S(1)} %slice.30), channel_id=7, replica_groups=mesh['grp'=16,'dom'=32] {'grp'}, dimensions={0}, use_global_device_ids=true | all-gather | bytes 139264 | tf_op jit(solution)/shard_map/all_gather | solution.py:91
  338.9 81.1 %all-gather.22.cloned.1.call-done = f32[8192,256]{1,0:T(8,128)} async-done(((f32[256,256]{1,0:T(8,128)}), f32[8192,256]{1,0:T(8,128)}) %all-gather.22.cloned.1.call-update) | async-done | bytes 8388624 | tf_op jit(solution)/shard_map/all_gather | solution.py:11
  420.0 84.8 %all-gather.24.cloned.1.call-done = f32[8192,1,128]{2,1,0:T(1,128)} async-done(((f32[256,1,128]{2,1,0:T(1,128)}), f32[8192,1,128]{2,1,0:T(1,128)}) %all-gather.24.cloned.1.call-update) | async-done | bytes 4194320 | tf_op jit(solution)/shard_map/all_gather | solution.py:11
  504.9 43.8 %while.27 = (s32[]{:T(128)}, f32[256,128]{1,0:T(8,128)S(1)}, s32[]{:T(128)}, f32[32,256,256]{2,1,0:T(8,128)}, f32[32,256,128]{2,1,0:T(8,128)}, /*index=5*/s32[]{:T(128)}, s32[]{:T(128)}, s32[]{:T(128)}, s32[]{:T(128)}) while((s32[]{:T(128)}, f32[256,128]{1,0:T(8,128)S(1)}, s32[]{:T(128)}, f32[32,256,256]{2,1,0:T(8,128)}, ...), condition=%wide.region_5.6_spmd, body=%wide.region_4.5_spmd.sunk | while | flops 100696072 | bytes 918675 | solution.py:20
  504.9 1.4 convolution_add_fusion.5
  506.4 1.4 convolution_add_fusion.5
  507.8 1.4 convolution_add_fusion.5
  509.2 1.4 convolution_add_fusion.5
  510.6 1.4 convolution_add_fusion.5
  512.0 1.4 convolution_add_fusion.5
  513.4 1.4 convolution_add_fusion.5
  514.8 1.4 convolution_add_fusion.5
  516.3 1.4 convolution_add_fusion.5
  517.7 1.4 convolution_add_fusion.5
  519.1 1.4 convolution_add_fusion.5
  520.5 1.4 convolution_add_fusion.5
  521.9 1.4 convolution_add_fusion.5
  523.3 1.4 convolution_add_fusion.5
  524.7 1.4 convolution_add_fusion.5
  526.1 1.4 convolution_add_fusion.5
  527.6 1.4 convolution_add_fusion.5
  529.0 1.4 convolution_add_fusion.5
  530.4 1.4 convolution_add_fusion.5
  531.8 1.4 convolution_add_fusion.5
  533.2 1.4 convolution_add_fusion.5
  534.6 1.4 convolution_add_fusion.5
  536.0 1.4 convolution_add_fusion.5
  537.4 1.4 convolution_add_fusion.5
  538.9 1.4 convolution_add_fusion.5
  540.3 1.4 convolution_add_fusion.5
  541.7 1.4 convolution_add_fusion.5
  543.1 1.4 convolution_add_fusion.5
  544.5 1.4 convolution_add_fusion.5
  545.9 1.4 convolution_add_fusion.5
  547.3 1.4 convolution_add_fusion.5
  548.7 0.4 fusion.39
  549.1 0.9 fusion.35
  550.1 0.9 copy.28
  550.9 38.1 %all-gather.14.cloned.1.call-done = bf16[4096,128]{0,1:T(8,128)(2,1)} async-done(((bf16[256,128]{0,1:T(8,128)(2,1)}), bf16[4096,128]{0,1:T(8,128)(2,1)}) %all-gather.14.cloned.1.call-update) | async-done | bytes 1048592 | tf_op jit(solution)/shard_map/all_gather | solution.py:101
  589.0 1.6 copy.34
  590.6 3.2 gather_fusion
  593.8 1.4 fusion.27
  595.3 0.8 copy.35
  (60 shorter events, 1.2 us)
Async XLA Ops:
  6.5 1.6 copy-start
  6.5 119.6 %all-gather.16.cloned.1.call-start = ((), (), s32[]{:S(2)}) async-start(), calls=%async_computation.1 | async-start | bytes 17825792 | tf_op jit(solution)/shard_map/all_gather | solution.py:59
  20.0 209.1 %all-gather.18.cloned.1.call-start = ((), (), s32[]{:S(2)}) async-start(), calls=%async_computation.2 | async-start | bytes 8650752 | tf_op jit(solution)/shard_map/all_gather | solution.py:11
  36.8 2.6 copy-start.1
  68.1 245.9 %all-gather.20.cloned.1.call-start = ((), (), s32[]{:S(2)}) async-start(), calls=%async_computation.3 | async-start | bytes 4325376 | tf_op jit(solution)/shard_map/all_gather | solution.py:11
  154.9 265.2 %all-gather.22.cloned.1.call-start = ((), (), s32[]{:S(2)}) async-start(), calls=%async_computation.4 | async-start | bytes 8650752 | tf_op jit(solution)/shard_map/all_gather | solution.py:11
  173.1 331.8 %all-gather.24.cloned.1.call-start = ((), (), s32[]{:S(2)}) async-start(), calls=%async_computation.5 | async-start | bytes 4325376 | tf_op jit(solution)/shard_map/all_gather | solution.py:11
  338.7 250.3 %all-gather.14.cloned.1.call-start = ((), (), s32[]{:S(2)}) async-start(), calls=%async_computation | async-start | bytes 1114112 | tf_op jit(solution)/shard_map/all_gather | solution.py:101
  504.8 43.9 %copy-start.2 = (f32[1,256,256]{2,1,0:T(8,128)S(1)}, f32[1,256,256]{2,1,0:T(8,128)}, u32[]{:S(2)}) copy-start(f32[1,256,256]{2,1,0:T(8,128)} %param.15) | copy-start | bytes 786436
  504.8 45.2 %copy-start.3 = (bf16[1,1,1024,128]{3,2,1,0:T(8,128)(2,1)S(1)}, bf16[1,1,1024,128]{3,2,1,0:T(8,128)(2,1)}, u32[]{:S(2)}) copy-start(bf16[1,1,1024,128]{3,2,1,0:T(8,128)(2,1)} %param.10) | copy-start | bytes 786436
Sparse Core Ops, SparseCore 0:
  20.1 106.0 all-gather.15
  129.4 99.6 all-gather.17
  232.3 81.7 all-gather.19
  317.1 102.9 all-gather.21
  423.1 81.7 all-gather.23
  550.2 38.7 all-gather.13
